TPU v7x, 256 devices: a whole 4x4x8 slice. The times are simulated.
256 devices in a mesh: seq: 32 (over x, z), head: 8 (over y, core).
Axes of the slice: x: 4, y: 4, z: 8, core: 2. Of those that a mesh axis runs over, the one named last changes fastest.
Arguments:
- tokens: bfloat16 [8192, 3072], P('seq', 'head'), may hold values from -6 to 6
- norm_gain: float32 [3072], replicated, may hold values from 0.1 to 1.9
- w_query: bfloat16 [3072, 3072], P(None, 'head'), may hold values from -0.109375 to 0.109375
- w_key: bfloat16 [3072, 1024], P(None, 'head'), may hold values from -0.3125 to 0.3125
- w_value: bfloat16 [3072, 1024], P(None, 'head'), may hold values from -0.109375 to 0.109375
- w_out: bfloat16 [3072, 3072], P('head'), may hold values from -0.109375 to 0.109375
- keys_cache: bfloat16 [65536, 1024], P('seq', 'head'), may hold values from -120 to 120
- values_cache: bfloat16 [65536, 1024], P('seq', 'head'), may hold values from -6 to 6
- cached_lengths: int32 [4], replicated, may hold values from 0 to 14336, as said below
- rope_offsets: int32 [4], replicated, may hold values from 0 to 8191
Outputs:
- attn_proj: bfloat16 [8192, 3072], P('seq', 'head')
- keys_updated: bfloat16 [65536, 1024], P('seq', 'head')
- values_updated: bfloat16 [65536, 1024], P('seq', 'head')
Inputs may be any that keep to these rules, and one draw needn't show every extreme that they name: `cached_lengths`: in every draw one request has exactly 14336 cached tokens.
All inputs are finite; a program needn't handle non-finite values.
Results may differ from a plain program's by a relative error of at most 0.02.
Values may be sent and summed in bfloat16 or wider, within the bound.
A program may use at most 128 MiB of HBM per device.

v0:
```python
import math
import jax
import jax.numpy as jnp
from jax import lax
from jax.sharding import PartitionSpec as P

HD = 128
rope_base = 500000.0
neg_large = -1e30


def shifted(shard, axis, by):
    devices = lax.axis_size(axis)
    return lax.ppermute(shard, axis, [(i, (i + by) % devices) for i in range(devices)])


def rotate(vectors, positions):
    half_width = vectors.shape[-1] // 2
    frequency = rope_base ** (-jnp.arange(half_width, dtype=jnp.float32) * 2.0 / vectors.shape[-1])
    angles = positions.astype(jnp.float32)[:, None] * frequency[None, :]
    cosine = jnp.cos(angles)[:, None, :]
    sine_part = jnp.sin(angles)[:, None, :]
    first_half = vectors[..., :half_width]
    second_half = vectors[..., half_width:]
    return jnp.concatenate(
        [
            first_half * cosine - second_half * sine_part,
            second_half * cosine + first_half * sine_part,
        ],
        -1,
    )


def shards(
    tokens,
    norm_gain,
    w_query,
    w_key,
    w_value,
    w_out,
    keys_cache,
    values_cache,
    cached_lengths,
    rope_offsets,
):
    gathered = lax.all_gather(tokens, "head", axis=1, tiled=True)
    row_count = gathered.shape[0]
    requests = cached_lengths.shape[0]
    groups = lax.axis_size("seq") // requests
    member = lax.axis_index("seq")
    request = member % requests
    position_in = member // requests
    length = lax.dynamic_index_in_dim(cached_lengths, request, 0, False)
    offset = lax.dynamic_index_in_dim(rope_offsets, request, 0, False)
    widened = gathered.astype(jnp.float32)
    normed = (
        widened * lax.rsqrt(jnp.mean(widened * widened, -1, keepdims=True) + 1e-05) * norm_gain
    ).astype(jnp.bfloat16)
    index_new = position_in * row_count + jnp.arange(row_count, dtype=jnp.int32)
    positions = offset + length + index_new
    kv_heads = w_key.shape[1] // HD
    q_heads = w_query.shape[1] // HD
    repeat = q_heads // kv_heads
    queries = rotate(
        jnp.dot(normed, w_query, preferred_element_type=jnp.float32).reshape(
            row_count, q_heads, HD
        ),
        positions,
    ).astype(jnp.bfloat16)
    new_keys = (
        rotate(
            jnp.dot(normed, w_key, preferred_element_type=jnp.float32).reshape(
                row_count, kv_heads, HD
            ),
            positions,
        )
        .astype(jnp.bfloat16)
        .reshape(row_count, kv_heads * HD)
    )
    new_values = jnp.dot(normed, w_value, preferred_element_type=jnp.float32).astype(jnp.bfloat16)
    grouped = (
        queries.reshape(row_count, kv_heads, repeat, HD)
        .transpose(1, 2, 0, 3)
        .reshape(kv_heads, repeat * row_count, HD)
    )
    slab_rows = keys_cache.shape[0]
    score_scale = 1.0 / math.sqrt(HD)

    def attend(softmax_state, query_group, key_block, value_block, visible):
        running_max, denominator, accumulated = softmax_state
        scores = (
            jnp.einsum(
                "gqd,kgd->gqk",
                query_group,
                key_block.reshape(-1, kv_heads, HD),
                preferred_element_type=jnp.float32,
            )
            * score_scale
        )
        masked = jnp.where(visible, scores, neg_large)
        new_max = jnp.maximum(running_max, jnp.max(masked, -1))
        weights = jnp.where(visible, jnp.exp(masked - new_max[..., None]), 0.0)
        factor = jnp.exp(running_max - new_max)
        denominator = denominator * factor + jnp.sum(weights, -1)
        accumulated = accumulated * factor[..., None] + jnp.einsum(
            "gqk,kgd->gqd",
            weights.astype(jnp.bfloat16),
            value_block.reshape(-1, kv_heads, HD),
            preferred_element_type=jnp.float32,
        )
        return (new_max, denominator, accumulated)

    def attend_pair(
        softmax_state,
        query_anchor,
        query_group,
        slab_keys,
        slab_values,
        slab_source,
        fresh_keys,
        fresh_values,
        fresh_source,
    ):
        query_index = jnp.tile(
            query_anchor * row_count + jnp.arange(row_count, dtype=jnp.int32), repeat
        )
        slots = slab_source * slab_rows + jnp.arange(slab_rows, dtype=jnp.int32)
        old_visible = (slots < length)[None, None, :]
        fresh_index = fresh_source * row_count + jnp.arange(row_count, dtype=jnp.int32)
        fresh_visible = (fresh_index[None, :] <= query_index[:, None])[None]
        softmax_state = attend(softmax_state, query_group, slab_keys, slab_values, old_visible)
        softmax_state = attend(softmax_state, query_group, fresh_keys, fresh_values, fresh_visible)
        return softmax_state

    def write_fresh(out_keys, out_values, fresh_keys, fresh_values, fresh_source):
        fresh_index = fresh_source * row_count + jnp.arange(row_count, dtype=jnp.int32)
        local_slot = length + fresh_index - position_in * slab_rows
        target = jnp.where((local_slot >= 0) & (local_slot < slab_rows), local_slot, slab_rows)
        out_keys = out_keys.at[target].set(fresh_keys, mode="drop")
        out_values = out_values.at[target].set(fresh_values, mode="drop")
        return (out_keys, out_values)

    def absorb(loop_carry, incoming, source):
        softmax_state, out_keys, out_values = loop_carry
        fresh_keys = incoming[0, slab_rows:]
        fresh_values = incoming[1, slab_rows:]
        softmax_state = attend_pair(
            softmax_state,
            position_in,
            grouped,
            incoming[0, :slab_rows],
            incoming[1, :slab_rows],
            source,
            fresh_keys,
            fresh_values,
            source,
        )
        out_keys, out_values = write_fresh(out_keys, out_values, fresh_keys, fresh_values, source)
        return (softmax_state, out_keys, out_values)

    start_state = (
        jnp.full((kv_heads, repeat * row_count), neg_large, jnp.float32),
        jnp.zeros((kv_heads, repeat * row_count), jnp.float32),
        jnp.zeros((kv_heads, repeat * row_count, HD), jnp.float32),
    )
    outgoing = jnp.stack(
        [
            jnp.concatenate([keys_cache, new_keys], 0),
            jnp.concatenate([values_cache, new_values], 0),
        ],
        0,
    )
    loop_carry = absorb((start_state, keys_cache, values_cache), outgoing, position_in)

    def cycle_step(cycle_turn, cycle_carry):
        held_blocks, inner_carry = cycle_carry
        held_blocks = shifted(held_blocks, "seq", requests)
        source = (position_in - cycle_turn) % groups
        return (held_blocks, absorb(inner_carry, held_blocks, source))

    unused, loop_carry = lax.fori_loop(1, groups, cycle_step, (outgoing, loop_carry))
    final_state, keys_updated, values_updated = loop_carry
    running_max, denominator, accumulated = final_state
    attended = (
        (accumulated / denominator[..., None])
        .reshape(kv_heads, repeat, row_count, HD)
        .transpose(2, 0, 1, 3)
        .reshape(row_count, q_heads * HD)
        .astype(jnp.bfloat16)
    )
    partial_value = jnp.dot(attended, w_out, preferred_element_type=jnp.float32)
    summed = lax.psum(partial_value.astype(jnp.bfloat16), "head").astype(jnp.float32)
    share_width = partial_value.shape[1] // lax.axis_size("head")
    projected = lax.dynamic_slice_in_dim(
        summed, lax.axis_index("head") * share_width, share_width, 1
    )
    return (projected.astype(jnp.bfloat16), keys_updated, values_updated)


def solution(mesh):
    return jax.shard_map(
        shards,
        mesh=mesh,
        in_specs=(
            P("seq", "head"),
            P(),
            P(None, "head"),
            P(None, "head"),
            P(None, "head"),
            P("head", None),
            P("seq", "head"),
            P("seq", "head"),
            P(),
            P(),
        ),
        out_specs=(P("seq", "head"), P("seq", "head"), P("seq", "head")),
        check_vma=False,
    )
```

profile of v0, /device:TPU:2, one launch (start us, length us, event | category | flops | bytes accessed | tf_op | source)
XLA Modules:
  0.0 639.8 jit_solution(14705658243390205139)
XLA Ops:
  17.2 23.6 %all-gather.2.cloned.1.call-done = bf16[256,3072]{1,0:T(8,128)(2,1)} async-done(((bf16[256,384]{1,0:T(8,128)(2,1)}), bf16[256,3072]{1,0:T(8,128)(2,1)}) %all-gather.2.cloned.1.call-update) | async-done | bytes 1572880 | tf_op jit(solution)/shard_map/all_gather | solution.py:46
  49.5 3.2 scatter_custom_fusion.2
  53.9 3.2 scatter_custom_fusion.3
  57.1 3.3 fusion.81
  71.4 386.1 %while.25 = (s32[]{:T(128)}, bf16[2,2304,128]{2,1,0:T(8,128)(2,1)}, f32[1,768]{1,0:T(1,128)S(1)}, f32[1,768]{1,0:T(1,128)}, f32[1,768,128]{2,1,0:T(8,128)}, /*in...) while((s32[]{:T(128)}, bf16[2,2304,128]{2,1,0:T(8,128)(2,1)}, ...), condition=%wide.region_14.15_spmd, body=%wide.region_7.14_spmd.sunk | while | flops 929181184 | bytes 57951692 | solution.py:181
  71.4 5.7 collective-permute-start
  79.0 41.7 %collective-permute-done = bf16[2,2304,128]{2,1,0:T(8,128)(2,1)S(1)} collective-permute-done((bf16[2,2304,128]{2,1,0:T(8,128)(2,1)}, bf16[2,2304,128]{2,1,0:T(8,128)(2,1)S(1)}, u32[]{:S(2)}, u32[]{:S(2)}) %collective-permute-start) | collective-permute-done | bytes 1179680 | tf_op jit(solution)/shard_map/while/body/eval_jaxpr/ppermute | solution.py:14
  135.8 5.2 fusion.109
  141.0 5.1 collective-permute-start
  148.0 23.2 %collective-permute-done = bf16[2,2304,128]{2,1,0:T(8,128)(2,1)S(1)} collective-permute-done((bf16[2,2304,128]{2,1,0:T(8,128)(2,1)}, bf16[2,2304,128]{2,1,0:T(8,128)(2,1)S(1)}, u32[]{:S(2)}, u32[]{:S(2)}) %collective-permute-start) | collective-permute-done | bytes 1179680 | tf_op jit(solution)/shard_map/while/body/eval_jaxpr/ppermute | solution.py:14
  186.4 5.2 fusion.109
  191.5 4.2 collective-permute-start
  197.6 27.7 %collective-permute-done = bf16[2,2304,128]{2,1,0:T(8,128)(2,1)S(1)} collective-permute-done((bf16[2,2304,128]{2,1,0:T(8,128)(2,1)}, bf16[2,2304,128]{2,1,0:T(8,128)(2,1)S(1)}, u32[]{:S(2)}, u32[]{:S(2)}) %collective-permute-start) | collective-permute-done | bytes 1179680 | tf_op jit(solution)/shard_map/while/body/eval_jaxpr/ppermute | solution.py:14
  240.5 5.2 fusion.109
  249.1 29.3 %collective-permute-done = bf16[2,2304,128]{2,1,0:T(8,128)(2,1)S(1)} collective-permute-done((bf16[2,2304,128]{2,1,0:T(8,128)(2,1)}, bf16[2,2304,128]{2,1,0:T(8,128)(2,1)S(1)}, u32[]{:S(2)}, u32[]{:S(2)}) %collective-permute-start) | collective-permute-done | bytes 1179680 | tf_op jit(solution)/shard_map/while/body/eval_jaxpr/ppermute | solution.py:14
  293.6 5.2 fusion.109
  303.4 27.8 %collective-permute-done = bf16[2,2304,128]{2,1,0:T(8,128)(2,1)S(1)} collective-permute-done((bf16[2,2304,128]{2,1,0:T(8,128)(2,1)}, bf16[2,2304,128]{2,1,0:T(8,128)(2,1)S(1)}, u32[]{:S(2)}, u32[]{:S(2)}) %collective-permute-start) | collective-permute-done | bytes 1179680 | tf_op jit(solution)/shard_map/while/body/eval_jaxpr/ppermute | solution.py:14
  346.4 5.2 fusion.109
  351.5 3.2 collective-permute-start
  356.7 27.8 %collective-permute-done = bf16[2,2304,128]{2,1,0:T(8,128)(2,1)S(1)} collective-permute-done((bf16[2,2304,128]{2,1,0:T(8,128)(2,1)}, bf16[2,2304,128]{2,1,0:T(8,128)(2,1)S(1)}, u32[]{:S(2)}, u32[]{:S(2)}) %collective-permute-start) | collective-permute-done | bytes 1179680 | tf_op jit(solution)/shard_map/while/body/eval_jaxpr/ppermute | solution.py:14
  399.7 5.2 fusion.109
  409.3 27.8 %collective-permute-done = bf16[2,2304,128]{2,1,0:T(8,128)(2,1)S(1)} collective-permute-done((bf16[2,2304,128]{2,1,0:T(8,128)(2,1)}, bf16[2,2304,128]{2,1,0:T(8,128)(2,1)S(1)}, u32[]{:S(2)}, u32[]{:S(2)}) %collective-permute-start) | collective-permute-done | bytes 1179680 | tf_op jit(solution)/shard_map/while/body/eval_jaxpr/ppermute | solution.py:14
  452.3 5.2 fusion.109
  461.7 169.6 %all-reduce.2.cloned.1.call-done = bf16[256,3072]{1,0:T(8,128)(2,1)} async-done(((bf16[256,3072]{1,0:T(8,128)(2,1)}), bf16[256,3072]{1,0:T(8,128)(2,1)}) %all-reduce.2.cloned.1.call-update) | async-done | bytes 1572880 | tf_op jit(solution)/shard_map/psum | solution.py:192
  (219 shorter events, 161.0 us)
Async XLA Ops:
  7.2 452.3 %copy-start = (bf16[384,3072]{1,0:T(8,128)(2,1)S(1)}, bf16[384,3072]{1,0:T(8,128)(2,1)}, u32[]{:S(2)}) copy-start(bf16[384,3072]{1,0:T(8,128)(2,1)} %param.17) | copy-start | bytes 7077892
  7.2 36.1 %copy-start.9 = (f32[3072]{0:T(1024)S(1)}, f32[3072]{0:T(1024)}, u32[]{:S(2)}) copy-start(f32[3072]{0:T(1024)} %param.13) | copy-start | bytes 36868
  7.2 33.6 %all-gather.2.cloned.1.call-start = ((), (), s32[]{:S(2)}) async-start(), calls=%async_computation | async-start | bytes 1769472 | tf_op jit(solution)/shard_map/all_gather | solution.py:46
  8.4 37.7 %copy-start.2 = (bf16[2048,128]{1,0:T(8,128)(2,1)}, bf16[2048,128]{1,0:T(8,128)(2,1)S(1)}, u32[]{:S(2)}) copy-start(bf16[2048,128]{1,0:T(8,128)(2,1)S(1)} %copy.52) | copy-start | bytes 1572868
  10.5 620.8 %all-reduce.2.cloned.1.call-start = ((), (), s32[]{:S(2)}) async-start(), calls=%async_computation.1 | async-start | bytes 3145728 | tf_op jit(solution)/shard_map/psum | solution.py:192
  48.4 8.6 %copy-start.8 = (f32[256]{0:T(256)S(1)}, f32[256]{0:T(256)}, u32[]{:S(2)}) copy-start(f32[256]{0:T(256)} %copy-done.7) | copy-start | bytes 3076
  57.1 3.4 copy-start.3
  57.1 3.4 copy-start.4
  71.4 49.3 %collective-permute-start = (bf16[2,2304,128]{2,1,0:T(8,128)(2,1)}, bf16[2,2304,128]{2,1,0:T(8,128)(2,1)S(1)}, u32[]{:S(2)}, u32[]{:S(2)}) collective-permute-start(bf16[2,2304,128]{2,1,0:T(8,128)(2,1)} %get-tuple-element.428), channel_id=1, source_target_pairs={{0,32},{8,40},{16,48},{24,56},{32,64},{40,72},{48,80},{56,88},{64,... | collective-permute-start | bytes 3538952 | tf_op jit(solution)/shard_map/while/body/eval_jaxpr/ppermute | solution.py:14
  122.8 4.2 copy-start.1
  125.4 1.8 copy-start.5
  141.0 30.2 %collective-permute-start = (bf16[2,2304,128]{2,1,0:T(8,128)(2,1)}, bf16[2,2304,128]{2,1,0:T(8,128)(2,1)S(1)}, u32[]{:S(2)}, u32[]{:S(2)}) collective-permute-start(bf16[2,2304,128]{2,1,0:T(8,128)(2,1)} %get-tuple-element.428), channel_id=1, source_target_pairs={{0,32},{8,40},{16,48},{24,56},{32,64},{40,72},{48,80},{56,88},{64,... | collective-permute-start | bytes 3538952 | tf_op jit(solution)/shard_map/while/body/eval_jaxpr/ppermute | solution.py:14
  173.3 4.2 copy-start.1
  175.9 1.8 copy-start.5
  191.5 33.8 %collective-permute-start = (bf16[2,2304,128]{2,1,0:T(8,128)(2,1)}, bf16[2,2304,128]{2,1,0:T(8,128)(2,1)S(1)}, u32[]{:S(2)}, u32[]{:S(2)}) collective-permute-start(bf16[2,2304,128]{2,1,0:T(8,128)(2,1)} %get-tuple-element.428), channel_id=1, source_target_pairs={{0,32},{8,40},{16,48},{24,56},{32,64},{40,72},{48,80},{56,88},{64,... | collective-permute-start | bytes 3538952 | tf_op jit(solution)/shard_map/while/body/eval_jaxpr/ppermute | solution.py:14
  227.4 4.2 copy-start.1
  245.7 32.8 %collective-permute-start = (bf16[2,2304,128]{2,1,0:T(8,128)(2,1)}, bf16[2,2304,128]{2,1,0:T(8,128)(2,1)S(1)}, u32[]{:S(2)}, u32[]{:S(2)}) collective-permute-start(bf16[2,2304,128]{2,1,0:T(8,128)(2,1)} %get-tuple-element.428), channel_id=1, source_target_pairs={{0,32},{8,40},{16,48},{24,56},{32,64},{40,72},{48,80},{56,88},{64,... | collective-permute-start | bytes 3538952 | tf_op jit(solution)/shard_map/while/body/eval_jaxpr/ppermute | solution.py:14
  280.5 4.2 copy-start.1
  298.8 32.5 %collective-permute-start = (bf16[2,2304,128]{2,1,0:T(8,128)(2,1)}, bf16[2,2304,128]{2,1,0:T(8,128)(2,1)S(1)}, u32[]{:S(2)}, u32[]{:S(2)}) collective-permute-start(bf16[2,2304,128]{2,1,0:T(8,128)(2,1)} %get-tuple-element.428), channel_id=1, source_target_pairs={{0,32},{8,40},{16,48},{24,56},{32,64},{40,72},{48,80},{56,88},{64,... | collective-permute-start | bytes 3538952 | tf_op jit(solution)/shard_map/while/body/eval_jaxpr/ppermute | solution.py:14
  333.3 4.2 copy-start.1
  351.5 33.0 %collective-permute-start = (bf16[2,2304,128]{2,1,0:T(8,128)(2,1)}, bf16[2,2304,128]{2,1,0:T(8,128)(2,1)S(1)}, u32[]{:S(2)}, u32[]{:S(2)}) collective-permute-start(bf16[2,2304,128]{2,1,0:T(8,128)(2,1)} %get-tuple-element.428), channel_id=1, source_target_pairs={{0,32},{8,40},{16,48},{24,56},{32,64},{40,72},{48,80},{56,88},{64,... | collective-permute-start | bytes 3538952 | tf_op jit(solution)/shard_map/while/body/eval_jaxpr/ppermute | solution.py:14
  386.6 4.2 copy-start.1
  404.8 32.3 %collective-permute-start = (bf16[2,2304,128]{2,1,0:T(8,128)(2,1)}, bf16[2,2304,128]{2,1,0:T(8,128)(2,1)S(1)}, u32[]{:S(2)}, u32[]{:S(2)}) collective-permute-start(bf16[2,2304,128]{2,1,0:T(8,128)(2,1)} %get-tuple-element.428), channel_id=1, source_target_pairs={{0,32},{8,40},{16,48},{24,56},{32,64},{40,72},{48,80},{56,88},{64,... | collective-permute-start | bytes 3538952 | tf_op jit(solution)/shard_map/while/body/eval_jaxpr/ppermute | solution.py:14
  439.2 4.2 copy-start.1
  (13 other events, 17.7 us)
Sparse Core Ops, SparseCore 0:
  10.6 30.1 all-gather.1
  461.8 169.4 all-reduce.1
where the time goes:
time: 642 us; the launch traced here: 640 us
  waiting for transfers between devices  399 us (62%)
  matrix products  84.8 us (13%)
  local copies, waits for them, and re-layouts  67 us (10%)
  other arithmetic  48 us (7%)
  starting transfers between devices  25.4 us (4%)
  between operations  15.5 us (2%)
    ppermute x7, waiting for transfers between devices, shifted(): lax.ppermute(shard, axis, [(i, (i + by) % devices) for i in range(devices)])  205 us
    psum x1, waiting for transfers between devices, shards(): lax.psum(partial_value.astype(jnp.bfloat16), 'head').astype(jnp.float32)  170 us
    dot_general x16, matrix products, attend(): jnp.einsum('gqk,kgd->gqd', weights.astype(jnp.bfloat16), value_block.resh...  46.8 us
    dot_general x16, matrix products, attend(): jnp.einsum('gqd,kgd->gqk', query_group, key_block.reshape(-1, kv_heads, H...  27.8 us
    scatter x8, local copies, waits for them, and re-layouts, write_fresh(): out_keys = out_keys.at[target].set(fresh_keys, mode='drop')  25.5 us
    scatter x8, local copies, waits for them, and re-layouts, write_fresh(): out_values = out_values.at[target].set(fresh_values, mode='drop')  25.5 us
    ppermute x7, starting transfers between devices, shifted(): lax.ppermute(shard, axis, [(i, (i + by) % devices) for i in range(devices)])  25.3 us
    all_gather x1, waiting for transfers between devices, shards(): gathered = lax.all_gather(tokens, 'head', axis=1, tiled=True)  23.6 us
  transfers between devices with their start and end apart: 9, of which 9 were waited for; matrix products, arithmetic and copies ran while one was open for 3% of the time, Pallas kernels for 0%

commit v1 on v0

--- a/solution.py
+++ b/solution.py
@@ -189,7 +189,9 @@
         .astype(jnp.bfloat16)
     )
     partial_value = jnp.dot(attended, w_out, preferred_element_type=jnp.float32)
-    summed = lax.psum(partial_value.astype(jnp.bfloat16), "head").astype(jnp.float32)
+    summed = jnp.sum(lax.all_gather(partial_value.astype(jnp.bfloat16), "head"), axis=0).astype(
+        jnp.float32
+    )
     share_width = partial_value.shape[1] // lax.axis_size("head")
     projected = lax.dynamic_slice_in_dim(
         summed, lax.axis_index("head") * share_width, share_width, 1

time: 642 us -> 652 us (1.016)
  other arithmetic: 48 us -> 56.8 us
    all_gather x0 -> x1, waiting for transfers between devices: none -> 170 us  [shards(): lax.all_gather(partial_value.astype(jnp.bfloat16), 'head')]
    psum x1 -> x0, waiting for transfers between devices: 170 us -> none  [shards(): lax.psum(partial_value.astype(jnp.bfloat16), 'head').astype(jnp.float32)]
    reduce_sum x0 -> x1, other arithmetic: none -> 8.77 us  [shards(): jnp.sum(lax.all_gather(partial_value.astype(jnp.bfloat16), 'head'), axis=0)]
where the time goes in v1:
time: 652 us; the launch traced here: 648 us
  waiting for transfers between devices  399 us (61%)
  matrix products  84.8 us (13%)
  local copies, waits for them, and re-layouts  66 us (10%)
  other arithmetic  56.8 us (9%)
  starting transfers between devices  25.6 us (4%)
  between operations  15.6 us (2%)
    ppermute x7, waiting for transfers between devices, shifted(): lax.ppermute(shard, axis, [(i, (i + by) % devices) for i in range(devices)])  205 us
    all_gather x1, waiting for transfers between devices, shards(): lax.all_gather(partial_value.astype(jnp.bfloat16), 'head')  170 us
    dot_general x16, matrix products, attend(): jnp.einsum('gqk,kgd->gqd', weights.astype(jnp.bfloat16), value_block.resh...  46.8 us
    dot_general x16, matrix products, attend(): jnp.einsum('gqd,kgd->gqk', query_group, key_block.reshape(-1, kv_heads, H...  27.8 us
    scatter x8, local copies, waits for them, and re-layouts, write_fresh(): out_values = out_values.at[target].set(fresh_values, mode='drop')  25.5 us
    ppermute x7, starting transfers between devices, shifted(): lax.ppermute(shard, axis, [(i, (i + by) % devices) for i in range(devices)])  25.5 us
    scatter x8, local copies, waits for them, and re-layouts, write_fresh(): out_keys = out_keys.at[target].set(fresh_keys, mode='drop')  24 us
    all_gather x1, waiting for transfers between devices, shards(): gathered = lax.all_gather(tokens, 'head', axis=1, tiled=True)  23.6 us
  transfers between devices with their start and end apart: 9, of which 9 were waited for; matrix products, arithmetic and copies ran while one was open for 3% of the time, Pallas kernels for 0%

profile of v1, /device:TPU:2, one launch (start us, length us, event | category | flops | bytes accessed | tf_op | source)
XLA Modules:
  0.0 648.4 jit_solution(15483770678290170352)
XLA Ops:
  17.1 23.6 %all-gather.4.cloned.1.call-done = bf16[256,3072]{1,0:T(8,128)(2,1)} async-done(((bf16[256,384]{1,0:T(8,128)(2,1)}), bf16[256,3072]{1,0:T(8,128)(2,1)}) %all-gather.4.cloned.1.call-update) | async-done | bytes 1572880 | tf_op jit(solution)/shard_map/all_gather | solution.py:46
  51.8 3.2 scatter_custom_fusion.3
  56.1 3.3 fusion.81
  70.4 386.1 %while.25 = (s32[]{:T(128)}, bf16[2,2304,128]{2,1,0:T(8,128)(2,1)}, f32[1,768]{1,0:T(1,128)S(1)}, f32[1,768]{1,0:T(1,128)}, f32[1,768,128]{2,1,0:T(8,128)}, /*in...) while((s32[]{:T(128)}, bf16[2,2304,128]{2,1,0:T(8,128)(2,1)}, ...), condition=%wide.region_14.15_spmd, body=%wide.region_7.14_spmd.sunk | while | flops 929181184 | bytes 57951692 | solution.py:181
  70.4 5.7 collective-permute-start
  78.0 41.6 %collective-permute-done = bf16[2,2304,128]{2,1,0:T(8,128)(2,1)S(1)} collective-permute-done((bf16[2,2304,128]{2,1,0:T(8,128)(2,1)}, bf16[2,2304,128]{2,1,0:T(8,128)(2,1)S(1)}, u32[]{:S(2)}, u32[]{:S(2)}) %collective-permute-start) | collective-permute-done | bytes 1179680 | tf_op jit(solution)/shard_map/while/body/eval_jaxpr/ppermute | solution.py:14
  134.8 5.2 fusion.109
  140.0 5.2 collective-permute-start
  147.0 23.2 %collective-permute-done = bf16[2,2304,128]{2,1,0:T(8,128)(2,1)S(1)} collective-permute-done((bf16[2,2304,128]{2,1,0:T(8,128)(2,1)}, bf16[2,2304,128]{2,1,0:T(8,128)(2,1)S(1)}, u32[]{:S(2)}, u32[]{:S(2)}) %collective-permute-start) | collective-permute-done | bytes 1179680 | tf_op jit(solution)/shard_map/while/body/eval_jaxpr/ppermute | solution.py:14
  185.3 5.2 fusion.109
  190.5 4.3 collective-permute-start
  196.7 27.7 %collective-permute-done = bf16[2,2304,128]{2,1,0:T(8,128)(2,1)S(1)} collective-permute-done((bf16[2,2304,128]{2,1,0:T(8,128)(2,1)}, bf16[2,2304,128]{2,1,0:T(8,128)(2,1)S(1)}, u32[]{:S(2)}, u32[]{:S(2)}) %collective-permute-start) | collective-permute-done | bytes 1179680 | tf_op jit(solution)/shard_map/while/body/eval_jaxpr/ppermute | solution.py:14
  239.5 5.2 fusion.109
  248.1 29.3 %collective-permute-done = bf16[2,2304,128]{2,1,0:T(8,128)(2,1)S(1)} collective-permute-done((bf16[2,2304,128]{2,1,0:T(8,128)(2,1)}, bf16[2,2304,128]{2,1,0:T(8,128)(2,1)S(1)}, u32[]{:S(2)}, u32[]{:S(2)}) %collective-permute-start) | collective-permute-done | bytes 1179680 | tf_op jit(solution)/shard_map/while/body/eval_jaxpr/ppermute | solution.py:14
  292.6 5.2 fusion.109
  302.5 27.7 %collective-permute-done = bf16[2,2304,128]{2,1,0:T(8,128)(2,1)S(1)} collective-permute-done((bf16[2,2304,128]{2,1,0:T(8,128)(2,1)}, bf16[2,2304,128]{2,1,0:T(8,128)(2,1)S(1)}, u32[]{:S(2)}, u32[]{:S(2)}) %collective-permute-start) | collective-permute-done | bytes 1179680 | tf_op jit(solution)/shard_map/while/body/eval_jaxpr/ppermute | solution.py:14
  345.4 5.2 fusion.109
  350.5 3.3 collective-permute-start
  355.7 27.8 %collective-permute-done = bf16[2,2304,128]{2,1,0:T(8,128)(2,1)S(1)} collective-permute-done((bf16[2,2304,128]{2,1,0:T(8,128)(2,1)}, bf16[2,2304,128]{2,1,0:T(8,128)(2,1)S(1)}, u32[]{:S(2)}, u32[]{:S(2)}) %collective-permute-start) | collective-permute-done | bytes 1179680 | tf_op jit(solution)/shard_map/while/body/eval_jaxpr/ppermute | solution.py:14
  398.7 5.2 fusion.109
  408.3 27.8 %collective-permute-done = bf16[2,2304,128]{2,1,0:T(8,128)(2,1)S(1)} collective-permute-done((bf16[2,2304,128]{2,1,0:T(8,128)(2,1)}, bf16[2,2304,128]{2,1,0:T(8,128)(2,1)S(1)}, u32[]{:S(2)}, u32[]{:S(2)}) %collective-permute-start) | collective-permute-done | bytes 1179680 | tf_op jit(solution)/shard_map/while/body/eval_jaxpr/ppermute | solution.py:14
  451.3 5.2 fusion.109
  460.7 170.4 %all-gather.6.cloned.1.call-done = bf16[2048,3072]{1,0:T(8,128)(2,1)} async-done(((bf16[256,3072]{1,0:T(8,128)(2,1)}), bf16[2048,3072]{1,0:T(8,128)(2,1)}) %all-gather.6.cloned.1.call-update) | async-done | bytes 12582928 | tf_op jit(solution)/shard_map/all_gather | solution.py:192
  631.2 8.8 %reduce_sum.74 = bf16[256,3072]{1,0:T(8,128)(2,1)} reduce(bf16[8,256,3072]{2,1,0:T(8,128)(2,1)} %bitcast.118, bf16[]{:T(256)} %constant.176.clone.1), dimensions={0}, to_apply=%region_15.16 | reduce | flops 5505024 | bytes 14155778 | tf_op jit(solution)/shard_map/reduce_sum | solution.py:192
  (220 shorter events, 163.4 us)
Async XLA Ops:
  7.2 451.3 %copy-start = (bf16[384,3072]{1,0:T(8,128)(2,1)S(1)}, bf16[384,3072]{1,0:T(8,128)(2,1)}, u32[]{:S(2)}) copy-start(bf16[384,3072]{1,0:T(8,128)(2,1)} %param.17) | copy-start | bytes 7077892
  7.2 35.9 %copy-start.9 = (f32[3072]{0:T(1024)S(1)}, f32[3072]{0:T(1024)}, u32[]{:S(2)}) copy-start(f32[3072]{0:T(1024)} %param.13) | copy-start | bytes 36868
  7.2 33.5 %all-gather.4.cloned.1.call-start = ((), (), s32[]{:S(2)}) async-start(), calls=%async_computation | async-start | bytes 1769472 | tf_op jit(solution)/shard_map/all_gather | solution.py:46
  10.3 620.8 %all-gather.6.cloned.1.call-start = ((), (), s32[]{:S(2)}) async-start(), calls=%async_computation.1 | async-start | bytes 14155776 | tf_op jit(solution)/shard_map/all_gather | solution.py:192
  48.4 7.7 %copy-start.8 = (f32[256]{0:T(256)S(1)}, f32[256]{0:T(256)}, u32[]{:S(2)}) copy-start(f32[256]{0:T(256)} %copy-done.7) | copy-start | bytes 3076
  56.1 3.4 copy-start.3
  56.1 3.4 copy-start.4
  70.4 49.2 %collective-permute-start = (bf16[2,2304,128]{2,1,0:T(8,128)(2,1)}, bf16[2,2304,128]{2,1,0:T(8,128)(2,1)S(1)}, u32[]{:S(2)}, u32[]{:S(2)}) collective-permute-start(bf16[2,2304,128]{2,1,0:T(8,128)(2,1)} %get-tuple-element.428), channel_id=1, source_target_pairs={{0,32},{8,40},{16,48},{24,56},{32,64},{40,72},{48,80},{56,88},{64,... | collective-permute-start | bytes 3538952 | tf_op jit(solution)/shard_map/while/body/eval_jaxpr/ppermute | solution.py:14
  121.7 4.5 copy-start.1
  126.2 2.2 copy-start.6
  140.0 30.2 %collective-permute-start = (bf16[2,2304,128]{2,1,0:T(8,128)(2,1)}, bf16[2,2304,128]{2,1,0:T(8,128)(2,1)S(1)}, u32[]{:S(2)}, u32[]{:S(2)}) collective-permute-start(bf16[2,2304,128]{2,1,0:T(8,128)(2,1)} %get-tuple-element.428), channel_id=1, source_target_pairs={{0,32},{8,40},{16,48},{24,56},{32,64},{40,72},{48,80},{56,88},{64,... | collective-permute-start | bytes 3538952 | tf_op jit(solution)/shard_map/while/body/eval_jaxpr/ppermute | solution.py:14
  172.3 4.5 copy-start.1
  176.8 2.2 copy-start.6
  190.5 33.8 %collective-permute-start = (bf16[2,2304,128]{2,1,0:T(8,128)(2,1)}, bf16[2,2304,128]{2,1,0:T(8,128)(2,1)S(1)}, u32[]{:S(2)}, u32[]{:S(2)}) collective-permute-start(bf16[2,2304,128]{2,1,0:T(8,128)(2,1)} %get-tuple-element.428), channel_id=1, source_target_pairs={{0,32},{8,40},{16,48},{24,56},{32,64},{40,72},{48,80},{56,88},{64,... | collective-permute-start | bytes 3538952 | tf_op jit(solution)/shard_map/while/body/eval_jaxpr/ppermute | solution.py:14
  226.4 4.5 copy-start.1
  230.9 2.2 copy-start.6
  244.7 32.8 %collective-permute-start = (bf16[2,2304,128]{2,1,0:T(8,128)(2,1)}, bf16[2,2304,128]{2,1,0:T(8,128)(2,1)S(1)}, u32[]{:S(2)}, u32[]{:S(2)}) collective-permute-start(bf16[2,2304,128]{2,1,0:T(8,128)(2,1)} %get-tuple-element.428), channel_id=1, source_target_pairs={{0,32},{8,40},{16,48},{24,56},{32,64},{40,72},{48,80},{56,88},{64,... | collective-permute-start | bytes 3538952 | tf_op jit(solution)/shard_map/while/body/eval_jaxpr/ppermute | solution.py:14
  279.5 4.5 copy-start.1
  297.8 32.4 %collective-permute-start = (bf16[2,2304,128]{2,1,0:T(8,128)(2,1)}, bf16[2,2304,128]{2,1,0:T(8,128)(2,1)S(1)}, u32[]{:S(2)}, u32[]{:S(2)}) collective-permute-start(bf16[2,2304,128]{2,1,0:T(8,128)(2,1)} %get-tuple-element.428), channel_id=1, source_target_pairs={{0,32},{8,40},{16,48},{24,56},{32,64},{40,72},{48,80},{56,88},{64,... | collective-permute-start | bytes 3538952 | tf_op jit(solution)/shard_map/while/body/eval_jaxpr/ppermute | solution.py:14
  332.3 4.5 copy-start.1
  350.5 33.0 %collective-permute-start = (bf16[2,2304,128]{2,1,0:T(8,128)(2,1)}, bf16[2,2304,128]{2,1,0:T(8,128)(2,1)S(1)}, u32[]{:S(2)}, u32[]{:S(2)}) collective-permute-start(bf16[2,2304,128]{2,1,0:T(8,128)(2,1)} %get-tuple-element.428), channel_id=1, source_target_pairs={{0,32},{8,40},{16,48},{24,56},{32,64},{40,72},{48,80},{56,88},{64,... | collective-permute-start | bytes 3538952 | tf_op jit(solution)/shard_map/while/body/eval_jaxpr/ppermute | solution.py:14
  385.6 4.5 copy-start.1
  403.8 32.3 %collective-permute-start = (bf16[2,2304,128]{2,1,0:T(8,128)(2,1)}, bf16[2,2304,128]{2,1,0:T(8,128)(2,1)S(1)}, u32[]{:S(2)}, u32[]{:S(2)}) collective-permute-start(bf16[2,2304,128]{2,1,0:T(8,128)(2,1)} %get-tuple-element.428), channel_id=1, source_target_pairs={{0,32},{8,40},{16,48},{24,56},{32,64},{40,72},{48,80},{56,88},{64,... | collective-permute-start | bytes 3538952 | tf_op jit(solution)/shard_map/while/body/eval_jaxpr/ppermute | solution.py:14
  438.2 4.5 copy-start.1
  (13 other events, 21.4 us)
Sparse Core Ops, SparseCore 0:
  10.4 30.1 all-gather.3
  460.8 170.2 all-gather.5
